TPU v7x, 1024 devices: a whole 4x4x32 slice. The times are simulated.
1024 devices in a mesh: gx: 16 (over z_hi, x, core), gy: 64 (over y, z_lo).
Axes of the slice: x: 4, y: 4, z: 32 (z_hi: 2, z_lo: 16; z = z_hi * 16 + z_lo), core: 2. Of those that a mesh axis runs over, the one named last changes fastest.
Arguments:
- density: float32 [1024, 256, 128], P('gx', 'gy'), may hold values from 0.8 to 1.2
- velocity: float32 [3, 1024, 256, 128], P(None, 'gx', 'gy'), may hold values from -1 to 1
- pressure: float32 [1024, 256, 128], P('gx', 'gy'), may hold values from 1.5 to 2.5
- disk_cells: int32 [16, 64, 512], P('gx', 'gy'), may hold values from 0 to 32767, as said below
- disk_count: int32 [16, 64], P('gx', 'gy'), may hold values from 0 to 512, as said below
- fringe_level: int32 [64], replicated, may hold values from 0 to 47
Outputs:
- conserved: float32 [5, 1024, 256, 128], P(None, 'gx', 'gy')
Inputs may be any that keep to these rules, and one draw needn't show every extreme that they name: `disk_cells`: distinct within each device block; slot k lies in [k * 64 * 4 * 128 // 512, (k + 1) * 64 * 4 * 128 // 512). `disk_count`: zero on the last device column (precursor); exactly 512 on some farm device block.
All inputs are finite; a program needn't handle non-finite values.
Results may differ from a plain program's by a relative error of at most 0.00002.
Values sent between devices are 32-bit elements; how exact they have to be, the bound alone decides.
A program may use at most 32 MiB of HBM per device.

v0:
```python
import jax
import jax.numpy as jnp
from jax import lax
from jax.sharding import PartitionSpec as P

TIME_STEP = 0.05
VISCOSITY = 0.5
THRUST_COEFF = 0.75
MEAN_WIND = 1.0


def padded_2(x, sides, width):
    for axis, dim in sides:
        size, length = (lax.axis_size(axis), x.shape[dim])
        up = [(i, (i + 1) % size) for i in range(size)]
        down = [(j, i) for i, j in up]
        last = lax.slice_in_dim(x, length - width, length, axis=dim)
        leading = lax.slice_in_dim(x, 0, width, axis=dim)
        before = lax.ppermute(last, axis, up)
        after = lax.ppermute(leading, axis, down)
        x = jnp.concatenate([before, x, after], axis=dim)
    return x


def from_behind(value, axis, steps):
    count = lax.axis_size(axis)
    leading, last = (max(0, -steps), min(count, count - steps))
    return lax.ppermute(value, axis, [(source, source + steps) for source in range(leading, last)])


def flux_along(fields, direction):
    density = fields[0]
    speeds = fields[1:4] / density
    pressure = 0.4 * (
        fields[4] - 0.5 * (fields[1] * speeds[0] + fields[2] * speeds[1] + fields[3] * speeds[2])
    )
    carried = speeds[direction]
    parts = [
        fields[1 + direction],
        fields[1] * carried,
        fields[2] * carried,
        fields[3] * carried,
        (fields[4] + pressure) * carried,
    ]
    parts[1 + direction] = parts[1 + direction] + pressure
    return jnp.stack(parts)


def vertical_pair(values):
    upper = jnp.concatenate([values[..., 1:], values[..., -1:]], axis=-1)
    lower = jnp.concatenate([values[..., :1], values[..., :-1]], axis=-1)
    return (upper, lower)


def add_terms(tendency_sum, fields, upper_flux, lower_flux, upper_cells, lower_cells):
    return (
        tendency_sum
        - 0.5 * (upper_flux - lower_flux)
        + VISCOSITY * (upper_cells + lower_cells - 2.0 * fields)
    )


def conserved_from(density, velocity, pressure):
    stream = velocity[0] + MEAN_WIND
    energy = pressure / 0.4 + 0.5 * density * (
        stream * stream + velocity[1] * velocity[1] + velocity[2] * velocity[2]
    )
    return jnp.stack(
        [density, density * stream, density * velocity[1], density * velocity[2], energy]
    )


def shards(density, velocity, pressure, disk_cells, disk_count, fringe_level):
    column = lax.axis_index("gx")
    column_count = lax.axis_size("gx")
    fields = conserved_from(density, velocity, pressure)
    stream_cells = fields.shape[1]
    cell_shape = fields.shape[1:]
    spots = disk_cells.reshape(-1)
    active = (jnp.arange(spots.shape[0], dtype=jnp.int32) < disk_count.reshape(())).astype(
        jnp.float32
    )
    weights = fringe_level.astype(jnp.float32) / 64.0
    fringe_width = fringe_level.shape[0]

    def tendency(state):
        padded = padded_2(state, (("gx", 1), ("gy", 2)), 1)
        last_plane = state[:, stream_cells - 1 :]
        first_plane = state[:, :1]
        lower_plane = jnp.where(column == column_count - 1, last_plane, padded[:, :1, 1:-1])
        upper_plane = jnp.where(
            column == column_count - 1,
            first_plane,
            jnp.where(column == column_count - 2, last_plane, padded[:, -1:, 1:-1]),
        )
        along_stream = jnp.concatenate([lower_plane, state, upper_plane], axis=1)
        along_span = padded[:, 1:-1]
        tendency_sum = jnp.zeros_like(state)
        moved = flux_along(along_stream, 0)
        tendency_sum = add_terms(
            tendency_sum,
            state,
            moved[:, 2:],
            moved[:, :-2],
            along_stream[:, 2:],
            along_stream[:, :-2],
        )
        moved = flux_along(along_span, 1)
        tendency_sum = add_terms(
            tendency_sum,
            state,
            moved[:, :, 2:],
            moved[:, :, :-2],
            along_span[:, :, 2:],
            along_span[:, :, :-2],
        )
        moved = flux_along(state, 2)
        upper_flux, lower_flux = vertical_pair(moved)
        upper_cells, lower_cells = vertical_pair(state)
        tendency_sum = add_terms(
            tendency_sum, state, upper_flux, lower_flux, upper_cells, lower_cells
        )
        rho_at = state[0].reshape(-1)[spots]
        stream_at = state[1].reshape(-1)[spots] / rho_at
        force = -0.5 * THRUST_COEFF * rho_at * stream_at * jnp.abs(stream_at) * active
        momentum = tendency_sum[1].reshape(-1).at[spots].add(force).reshape(cell_shape)
        energy = tendency_sum[4].reshape(-1).at[spots].add(force * stream_at).reshape(cell_shape)
        return jnp.stack([tendency_sum[0], momentum, tendency_sum[2], tendency_sum[3], energy])

    def blend(fresh):
        target = from_behind(fresh, "gx", 1 - column_count)
        ramp_weight = jnp.where(column == 0, weights, 0.0)
        blended = fresh + ramp_weight[None, :, None, None] * (target - fresh)
        return jnp.concatenate([blended, fresh[:, fringe_width:]], axis=1)

    first = blend(fields + TIME_STEP * tendency(fields))
    second = blend(0.75 * fields + 0.25 * (first + TIME_STEP * tendency(first)))
    fields = blend(fields / 3.0 + 2.0 / 3.0 * (second + TIME_STEP * tendency(second)))
    return fields


def solution(mesh):
    in_specs = (
        P("gx", "gy", None),
        P(None, "gx", "gy", None),
        P("gx", "gy", None),
        P("gx", "gy", None),
        P("gx", "gy"),
        P(),
    )
    out_specs = P(None, "gx", "gy", None)
    return jax.shard_map(shards, mesh=mesh, in_specs=in_specs, out_specs=out_specs, check_vma=False)
```

profile of v0, /device:TPU:56, one launch (start us, length us, event | category | flops | bytes accessed | tf_op | source)
XLA Modules:
  0.0 429.7 jit_solution(4137737596023303365)
XLA Ops:
  0.0 1.1 fusion.144
  1.1 0.9 copy.18
  2.2 0.8 copy-done.19
  3.2 29.7 %collective-permute-start.1 = (f32[5,1,4,128]{3,1,2,0:T(1,128)S(1)}, f32[5,1,4,128]{3,1,2,0:T(1,128)S(1)}, u32[]{:S(2)}, u32[]{:S(2)}) collective-permute-start(f32[5,1,4,128]{3,1,2,0:T(1,128)S(1)} %slice.723), channel_id=1, source_target_pairs={{64,0},{128,64},{192,128},{256,192},{320,256},{384,320},{448,384},... | collective-permute-start | bytes 30728 | tf_op jit(solution)/shard_map/ppermute | solution.py:20
  32.9 1.3 fusion.140
  34.2 1.9 fusion.141
  36.9 3.1 gather_fusion
  40.1 3.1 gather_fusion.1
  43.3 1.9 collective-permute-start
  45.2 23.7 %collective-permute-done = f32[5,1,4,128]{3,1,2,0:T(1,128)S(1)} collective-permute-done((f32[5,1,4,128]{3,1,2,0:T(1,128)S(1)}, f32[5,1,4,128]{3,1,2,0:T(1,128)S(1)}, u32[]{:S(2)}, u32[]{:S(2)}) %collective-permute-start) | collective-permute-done | bytes 10272 | tf_op jit(solution)/shard_map/ppermute | solution.py:19
  69.1 2.9 collective-permute-start.2
  72.0 3.0 collective-permute-start.3
  75.2 1.3 collective-permute-done.2
  76.6 2.9 collective-permute-done.3
  80.0 0.8 copy-done.5
  81.6 1.1 fusion.35
  82.9 0.7 copy-done.16
  83.6 4.1 scatter_fusion.1
  87.8 4.1 scatter_fusion
  92.0 1.3 collective-permute-start.4
  93.4 80.7 %collective-permute-done.4 = f32[5,64,4,128]{3,1,2,0:T(8,128)S(1)} collective-permute-done((f32[5,64,4,128]{3,1,2,0:T(8,128)S(1)}, f32[5,64,4,128]{3,1,2,0:T(8,128)S(1)}, u32[]{:S(2)}, u32[]{:S(2)}) %collective-permute-start.4) | collective-permute-done | bytes 655392 | tf_op jit(solution)/shard_map/ppermute | solution.py:28
  174.4 0.6 slice.764
  175.2 0.2 fusion.137
  175.5 1.1 fusion.138
  176.6 1.3 fusion.135
  177.8 1.9 collective-permute-start.6
  179.8 1.3 fusion.136
  181.1 4.3 %gather_fusion.2 = f32[512]{0:T(512)} fusion(f32[32768]{0:T(1024)S(1)} %bitcast.136, s32[1024]{0:T(1024)} %copy-done.20), kind=kCustom, calls=%fused_computation.2 | custom fusion | bytes 6144 | tf_op jit(solution)/shard_map/gather | solution.py:123
  185.6 3.3 gather_fusion.3
  188.9 2.4 collective-permute-start.5
  191.4 23.1 %collective-permute-done.5 = f32[5,1,4,128]{3,1,2,0:T(1,128)S(1)} collective-permute-done((f32[5,1,4,128]{3,1,2,0:T(1,128)S(1)}, f32[5,1,4,128]{3,1,2,0:T(1,128)S(1)}, u32[]{:S(2)}, u32[]{:S(2)}) %collective-permute-start.5) | collective-permute-done | bytes 10272 | tf_op jit(solution)/shard_map/ppermute | solution.py:19
  214.6 1.9 collective-permute-start.7
  216.6 4.1 collective-permute-start.8
  220.9 1.1 collective-permute-done.7
  222.1 1.9 collective-permute-done.8
  224.5 0.8 copy-done.15
  226.2 1.1 fusion.20
  227.4 0.7 copy-done.17
  228.1 4.1 scatter_fusion.3
  232.3 4.1 scatter_fusion.2
  236.7 1.3 collective-permute-start.9
  238.0 65.9 %collective-permute-done.9 = f32[5,64,4,128]{3,1,2,0:T(8,128)S(1)} collective-permute-done((f32[5,64,4,128]{3,1,2,0:T(8,128)S(1)}, f32[5,64,4,128]{3,1,2,0:T(8,128)S(1)}, u32[]{:S(2)}, u32[]{:S(2)}) %collective-permute-start.9) | collective-permute-done | bytes 655392 | tf_op jit(solution)/shard_map/ppermute | solution.py:28
  304.2 0.6 slice.811
  305.0 0.2 fusion.131
  305.3 1.1 fusion.132
  306.4 1.3 fusion.129
  307.6 1.9 collective-permute-start.11
  309.6 1.3 fusion.130
  310.9 4.3 %gather_fusion.4 = f32[512]{0:T(512)} fusion(f32[32768]{0:T(1024)S(1)} %bitcast.138, s32[1024]{0:T(1024)} %copy-done.20), kind=kCustom, calls=%fused_computation.4 | custom fusion | bytes 6144 | tf_op jit(solution)/shard_map/gather | solution.py:123
  315.4 3.3 gather_fusion.5
  318.7 2.4 collective-permute-start.10
  321.1 23.1 %collective-permute-done.10 = f32[5,1,4,128]{3,1,2,0:T(1,128)S(1)} collective-permute-done((f32[5,1,4,128]{3,1,2,0:T(1,128)S(1)}, f32[5,1,4,128]{3,1,2,0:T(1,128)S(1)}, u32[]{:S(2)}, u32[]{:S(2)}) %collective-permute-start.10) | collective-permute-done | bytes 10272 | tf_op jit(solution)/shard_map/ppermute | solution.py:19
  344.4 1.9 collective-permute-start.12
  346.4 3.9 collective-permute-start.13
  350.5 1.3 collective-permute-done.12
  351.9 1.9 collective-permute-done.13
  354.3 0.8 copy-done.13
  356.0 1.1 fusion.5
  357.2 0.7 copy-done.18
  357.9 4.1 scatter_fusion.5
  362.1 4.1 scatter_fusion.4
  366.5 1.3 collective-permute-start.14
  367.8 60.5 %collective-permute-done.14 = f32[5,64,4,128]{3,1,2,0:T(8,128)S(1)} collective-permute-done((f32[5,64,4,128]{3,1,2,0:T(8,128)S(1)}, f32[5,64,4,128]{3,1,2,0:T(8,128)S(1)}, u32[]{:S(2)}, u32[]{:S(2)}) %collective-permute-start.14) | collective-permute-done | bytes 655392 | tf_op jit(solution)/shard_map/ppermute | solution.py:28
  428.5 1.3 copy.45
  (162 shorter events, 8.3 us)
Async XLA Ops:
  0.0 2.0 copy-start
  2.1 0.9 copy-start.19
  3.2 40.0 %collective-permute-start.1 = (f32[5,1,4,128]{3,1,2,0:T(1,128)S(1)}, f32[5,1,4,128]{3,1,2,0:T(1,128)S(1)}, u32[]{:S(2)}, u32[]{:S(2)}) collective-permute-start(f32[5,1,4,128]{3,1,2,0:T(1,128)S(1)} %slice.723), channel_id=1, source_target_pairs={{64,0},{128,64},{192,128},{256,192},{320,256},{384,320},{448,384},... | collective-permute-start | bytes 30728 | tf_op jit(solution)/shard_map/ppermute | solution.py:20
  34.2 1.9 copy-start.26
  36.1 3.9 copy-start.20
  43.3 25.7 %collective-permute-start = (f32[5,1,4,128]{3,1,2,0:T(1,128)S(1)}, f32[5,1,4,128]{3,1,2,0:T(1,128)S(1)}, u32[]{:S(2)}, u32[]{:S(2)}) collective-permute-start(f32[5,1,4,128]{3,1,2,0:T(1,128)S(1)} %get-tuple-element.106), channel_id=1, source_target_pairs={{0,64},{64,128},{128,192},{192,256},{256,320},{320,384},{384,448},... | collective-permute-start | bytes 30728 | tf_op jit(solution)/shard_map/ppermute | solution.py:19
  69.1 7.4 %collective-permute-start.2 = (f32[5,66,1,128]{3,1,2,0:T(8,128)S(1)}, f32[5,66,1,128]{3,1,2,0:T(8,128)S(1)}, u32[]{:S(2)}, u32[]{:S(2)}) collective-permute-start(f32[5,66,1,128]{3,1,2,0:T(8,128)S(1)} %get-tuple-element.53), channel_id=1, source_target_pairs={{0,1},{1,2},{2,3},{3,4},{4,5},{5,6},{6,7},{7,8},{8,9},{9,10},{10,1... | collective-permute-start | bytes 506888 | tf_op jit(solution)/shard_map/ppermute | solution.py:19
  72.0 7.4 %collective-permute-start.3 = (f32[5,66,1,128]{3,1,2,0:T(8,128)S(1)}, f32[5,66,1,128]{3,1,2,0:T(8,128)S(1)}, u32[]{:S(2)}, u32[]{:S(2)}) collective-permute-start(f32[5,66,1,128]{3,1,2,0:T(8,128)S(1)} %get-tuple-element.52), channel_id=1, source_target_pairs={{1,0},{2,1},{3,2},{4,3},{5,4},{6,5},{7,6},{8,7},{9,8},{10,9},{11,1... | collective-permute-start | bytes 506888 | tf_op jit(solution)/shard_map/ppermute | solution.py:20
  79.7 1.1 copy-start.5
  79.7 1.3 copy-start.3
  79.8 1.4 copy-start.4
  79.9 1.5 copy-start.1
  79.9 1.7 copy-start.2
  82.8 0.8 copy-start.16
  87.8 4.1 slice-start
  91.9 1.5 copy-start.27
  92.0 82.1 %collective-permute-start.4 = (f32[5,64,4,128]{3,1,2,0:T(8,128)S(1)}, f32[5,64,4,128]{3,1,2,0:T(8,128)S(1)}, u32[]{:S(2)}, u32[]{:S(2)}) collective-permute-start(f32[5,64,4,128]{3,1,2,0:T(8,128)S(1)} %fusion.46), channel_id=1, source_target_pairs={{960,0},{961,1},{962,2},{963,3},{964,4},{965,5},{966,6},{967,7},{9... | collective-permute-start | bytes 1966088 | tf_op jit(solution)/shard_map/ppermute | solution.py:28
  93.4 81.6 %copy-start.23 = (f32[64]{0:T(128)}, f32[64]{0:T(128)S(1)}, u32[]{:S(2)}) copy-start(f32[64]{0:T(128)S(1)} %broadcast_select_fusion.9) | copy-start | bytes 772
  177.8 11.0 %collective-permute-start.6 = (f32[5,1,4,128]{3,1,2,0:T(1,128)}, f32[5,1,4,128]{3,1,2,0:T(1,128)S(1)}, u32[]{:S(2)}, u32[]{:S(2)}) collective-permute-start(f32[5,1,4,128]{3,1,2,0:T(1,128)} %slice.764), channel_id=1, source_target_pairs={{64,0},{128,64},{192,128},{256,192},{320,256},{384,320},{448,384},... | collective-permute-start | bytes 30728 | tf_op jit(solution)/shard_map/ppermute | solution.py:20
  185.6 5.8 %copy-start.22 = (f32[512]{0:T(512)S(1)}, f32[512]{0:T(512)}, u32[]{:S(2)}) copy-start(f32[512]{0:T(512)} %gather_fusion.2) | copy-start | bytes 6148
  188.9 25.5 %collective-permute-start.5 = (f32[5,1,4,128]{3,1,2,0:T(1,128)S(1)}, f32[5,1,4,128]{3,1,2,0:T(1,128)S(1)}, u32[]{:S(2)}, u32[]{:S(2)}) collective-permute-start(f32[5,1,4,128]{3,1,2,0:T(1,128)S(1)} %get-tuple-element.91), channel_id=1, source_target_pairs={{0,64},{64,128},{128,192},{192,256},{256,320},{320,384},{384,448},... | collective-permute-start | bytes 30728 | tf_op jit(solution)/shard_map/ppermute | solution.py:19
  214.6 7.4 %collective-permute-start.7 = (f32[5,66,1,128]{3,1,2,0:T(8,128)S(1)}, f32[5,66,1,128]{3,1,2,0:T(8,128)S(1)}, u32[]{:S(2)}, u32[]{:S(2)}) collective-permute-start(f32[5,66,1,128]{3,1,2,0:T(8,128)S(1)} %get-tuple-element.49), channel_id=1, source_target_pairs={{0,1},{1,2},{2,3},{3,4},{4,5},{5,6},{6,7},{7,8},{8,9},{9,10},{10,1... | collective-permute-start | bytes 506888 | tf_op jit(solution)/shard_map/ppermute | solution.py:19
  216.6 7.4 %collective-permute-start.8 = (f32[5,66,1,128]{3,1,2,0:T(8,128)S(1)}, f32[5,66,1,128]{3,1,2,0:T(8,128)S(1)}, u32[]{:S(2)}, u32[]{:S(2)}) collective-permute-start(f32[5,66,1,128]{3,1,2,0:T(8,128)S(1)} %get-tuple-element.48), channel_id=1, source_target_pairs={{1,0},{2,1},{3,2},{4,3},{5,4},{6,5},{7,6},{8,7},{9,8},{10,9},{11,1... | collective-permute-start | bytes 506888 | tf_op jit(solution)/shard_map/ppermute | solution.py:20
  224.2 1.1 copy-start.15
  224.3 1.3 copy-start.11
  224.3 1.4 copy-start.14
  224.4 1.5 copy-start.9
  224.4 1.7 copy-start.10
  227.3 0.8 copy-start.17
  232.3 4.1 slice-start.1
  236.5 67.5 %copy-start.24 = (f32[64]{0:T(128)S(1)}, f32[64]{0:T(128)}, u32[]{:S(2)}) copy-start(f32[64]{0:T(128)} %copy-done.23) | copy-start | bytes 772
  236.7 67.2 %collective-permute-start.9 = (f32[5,64,4,128]{3,1,2,0:T(8,128)S(1)}, f32[5,64,4,128]{3,1,2,0:T(8,128)S(1)}, u32[]{:S(2)}, u32[]{:S(2)}) collective-permute-start(f32[5,64,4,128]{3,1,2,0:T(8,128)S(1)} %fusion.50), channel_id=1, source_target_pairs={{960,0},{961,1},{962,2},{963,3},{964,4},{965,5},{966,6},{967,7},{9... | collective-permute-start | bytes 1966088 | tf_op jit(solution)/shard_map/ppermute | solution.py:28
  307.6 11.0 %collective-permute-start.11 = (f32[5,1,4,128]{3,1,2,0:T(1,128)}, f32[5,1,4,128]{3,1,2,0:T(1,128)S(1)}, u32[]{:S(2)}, u32[]{:S(2)}) collective-permute-start(f32[5,1,4,128]{3,1,2,0:T(1,128)} %slice.811), channel_id=1, source_target_pairs={{64,0},{128,64},{192,128},{256,192},{320,256},{384,320},{448,384},... | collective-permute-start | bytes 30728 | tf_op jit(solution)/shard_map/ppermute | solution.py:20
  315.4 5.8 %copy-start.21 = (f32[512]{0:T(512)S(1)}, f32[512]{0:T(512)}, u32[]{:S(2)}) copy-start(f32[512]{0:T(512)} %gather_fusion.4) | copy-start | bytes 6148
  318.7 25.5 %collective-permute-start.10 = (f32[5,1,4,128]{3,1,2,0:T(1,128)S(1)}, f32[5,1,4,128]{3,1,2,0:T(1,128)S(1)}, u32[]{:S(2)}, u32[]{:S(2)}) collective-permute-start(f32[5,1,4,128]{3,1,2,0:T(1,128)S(1)} %get-tuple-element.72), channel_id=1, source_target_pairs={{0,64},{64,128},{128,192},{192,256},{256,320},{320,384},{384,448},... | collective-permute-start | bytes 30728 | tf_op jit(solution)/shard_map/ppermute | solution.py:19
  344.4 7.4 %collective-permute-start.12 = (f32[5,66,1,128]{3,1,2,0:T(8,128)S(1)}, f32[5,66,1,128]{3,1,2,0:T(8,128)S(1)}, u32[]{:S(2)}, u32[]{:S(2)}) collective-permute-start(f32[5,66,1,128]{3,1,2,0:T(8,128)S(1)} %get-tuple-element.45), channel_id=1, source_target_pairs={{0,1},{1,2},{2,3},{3,4},{4,5},{5,6},{6,7},{7,8},{8,9},{9,10},{10,1... | collective-permute-start | bytes 506888 | tf_op jit(solution)/shard_map/ppermute | solution.py:19
  346.4 7.4 %collective-permute-start.13 = (f32[5,66,1,128]{3,1,2,0:T(8,128)S(1)}, f32[5,66,1,128]{3,1,2,0:T(8,128)S(1)}, u32[]{:S(2)}, u32[]{:S(2)}) collective-permute-start(f32[5,66,1,128]{3,1,2,0:T(8,128)S(1)} %get-tuple-element.44), channel_id=1, source_target_pairs={{1,0},{2,1},{3,2},{4,3},{5,4},{6,5},{7,6},{8,7},{9,8},{10,9},{11,1... | collective-permute-start | bytes 506888 | tf_op jit(solution)/shard_map/ppermute | solution.py:20
  354.0 1.1 copy-start.13
  354.1 1.3 copy-start.8
  354.1 1.4 copy-start.12
  354.2 1.5 copy-start.6
  354.2 1.7 copy-start.7
  357.1 0.8 copy-start.18
  362.1 4.1 slice-start.2
  366.2 62.0 %copy-start.25 = (f32[64]{0:T(128)S(1)}, f32[64]{0:T(128)}, u32[]{:S(2)}) copy-start(f32[64]{0:T(128)} %copy-done.23) | copy-start | bytes 772
  366.5 61.8 %collective-permute-start.14 = (f32[5,64,4,128]{3,1,2,0:T(8,128)S(1)}, f32[5,64,4,128]{3,1,2,0:T(8,128)S(1)}, u32[]{:S(2)}, u32[]{:S(2)}) collective-permute-start(f32[5,64,4,128]{3,1,2,0:T(8,128)S(1)} %fusion.54), channel_id=1, source_target_pairs={{960,0},{961,1},{962,2},{963,3},{964,4},{965,5},{966,6},{967,7},{9... | collective-permute-start | bytes 1966088 | tf_op jit(solution)/shard_map/ppermute | solution.py:28
where the time goes:
time: 430 us
  waiting for transfers between devices  288 us (67%)
  starting transfers between devices  61.8 us (14%)
  local copies, waits for them, and re-layouts  46.4 us (11%)
  other arithmetic  32.1 us (7%)
    ppermute x3, waiting for transfers between devices, from_behind(): lax.ppermute(value, axis, [(source, source + steps) for source in range(l...  207 us
    ppermute x6, waiting for transfers between devices, padded_2(): before = lax.ppermute(last, axis, up)  73.7 us
    ppermute x6, starting transfers between devices, padded_2(): after = lax.ppermute(leading, axis, down)  44.5 us
    ppermute x6, starting transfers between devices, padded_2(): before = lax.ppermute(last, axis, up)  13.5 us
    scatter-add x3, other arithmetic, tendency(): tendency_sum[1].reshape(-1).at[spots].add(force).reshape(cell_shape)  12.3 us
    scatter-add x3, other arithmetic, tendency(): tendency_sum[4].reshape(-1).at[spots].add(force * stream_at)  12.2 us
    gather x3, local copies, waits for them, and re-layouts, tendency(): rho_at = state[0].reshape(-1)[spots]  11.8 us
    slice x10, local copies, waits for them, and re-layouts, vertical_pair(): lower = jnp.concatenate([values[..., :1], values[..., :-1]], axis=-1)  11 us
  transfers between devices with their start and end apart: 15, of which 12 were waited for; matrix products, arithmetic and copies ran while one was open for 7% of the time, Pallas kernels for 0%

commit v1 on v0

v1 whole, which is shorter than its diff:
```python
import jax
import jax.numpy as jnp
from jax import lax
from jax.experimental import pallas as pl
from jax.experimental.pallas import tpu as pltpu
from jax.sharding import PartitionSpec as P

TIME_STEP = 0.05
THRUST_COEFF = 0.75
MEAN_WIND = 1.0
MESH = pl.DeviceIdType.MESH

CX, CY, NZ, NF = 64, 4, 128, 5
HY = 3
ROWS = CY + 2 * HY
XT = CX // 8 + 2
EX = 8 * XT
LAST = 15
Z_LO = 16


def conserved_from(density, velocity, pressure):
    stream = velocity[0] + MEAN_WIND
    energy = pressure / 0.4 + 0.5 * density * (
        stream * stream + velocity[1] * velocity[1] + velocity[2] * velocity[2]
    )
    return jnp.stack(
        [density, density * stream, density * velocity[1], density * velocity[2], energy]
    )


def body(s_ref, d_ref, w_ref, o_ref, st, ax, bx, ay, by, rr, thrust, dn, ra, rb, rbl, rbr,
         local_sem, send_sem, recv_sem):
    gx, gy = lax.axis_index("gx"), lax.axis_index("gy")
    up, down = lax.rem(gy + 1, 64), lax.rem(gy + 63, 64)
    z_lo = lax.rem(gy, Z_LO)
    first_z, last_z = z_lo == 0, z_lo == Z_LO - 1
    has_right, has_left = gx <= LAST - 2, (gx >= 1) & (gx <= LAST - 1)
    from_left, from_right = (gx >= 1) & (gx <= LAST - 1), gx <= LAST - 2
    u0 = st.at[0, 0]
    p0 = st.at[1, 0]

    sends = []

    def remote(index, recv, src, dst, target):
        return pltpu.make_async_remote_copy(
            src_ref=src, dst_ref=dst, send_sem=send_sem.at[index], recv_sem=recv_sem.at[recv],
            device_id=target, device_id_type=MESH,
        )

    barrier = pltpu.get_barrier_semaphore()

    def tell(condition, device):
        @pl.when(condition)
        def _():
            pl.semaphore_signal(barrier, inc=1, device_id=device, device_id_type=MESH)

    always = gx >= 0
    is_source = gx == LAST
    is_a = (gx == 9) | (gx == 11) | (gx == 13)
    is_b = (gx == 1) | (gx == 3) | (gx == 5) | (gx == 7)
    tell(is_b & (gx == 7), (LAST + 0 * gx, gy))
    tell(is_b & (gx != 7), (gx + 8, gy))
    tell((gx == 7) & first_z, (LAST + 0 * gx, down))
    tell(((gx == 3) | (gx == 5)) & first_z, (gx + 8, down))
    tell(((gx == 1) | (gx == 3) | (gx == 5)) & last_z, (gx + 8, up))
    tell(always, (gx, up))
    tell(always, (gx, down))
    for near in (gy, up, down):
        tell(from_left, (gx - 1, near))
        tell(from_right, (gx + 1, near))
    tell(is_a, (LAST + 0 * gx, gy))
    for c in range(4):
        tell(gx == 0, (1 + 2 * c + 0 * gx, gy))
        if c >= 1:
            tell((gx == 0) & jnp.logical_not(first_z), (1 + 2 * c + 0 * gx, down))
        if c <= 2:
            tell((gx == 0) & jnp.logical_not(last_z), (1 + 2 * c + 0 * gx, up))

    own = pltpu.make_async_copy(s_ref, u0.at[pl.ds(HY, CY), :, pl.ds(8, CX)], local_sem)
    own.start()

    def yes(condition):
        return jnp.where(condition, 1, 0)

    expected = 2 + 3 * yes(has_right) + 3 * yes(has_left)
    expected += yes(is_source) * (4 + yes(last_z))
    expected += yes(is_a) * (1 + yes(first_z)) + yes((gx == 11) | (gx == 13)) * yes(last_z)
    expected += yes(is_b)
    expected += yes((gx >= 3) & is_b) * yes(jnp.logical_not(last_z))
    expected += yes((gx <= 5) & is_b) * yes(jnp.logical_not(first_z))
    pl.semaphore_wait(barrier, expected)

    def send(condition, copy):
        sends.append((condition, copy))

        @pl.when(condition)
        def _():
            copy.start()

    send(is_source, remote(16, 17, s_ref.at[3], rb, (7 + 0 * gx, gy)))
    for c in range(3):
        send(is_source, remote(17 + c, 16, s_ref.at[c], ra, (9 + 2 * c + 0 * gx, gy)))
    send(is_source & last_z, remote(20, 18, s_ref.at[3], rbl, (7 + 0 * gx, up)))

    lo8, hi8 = pl.ds(0, 8), pl.ds(CX - 8, 8)
    left8, right8, mid = pl.ds(0, 8), pl.ds(EX - 8, 8), pl.ds(8, CX)
    halo = [
        (always, s_ref.at[pl.ds(1, 3)], u0.at[pl.ds(0, 3), :, mid], (gx, up), always, (0, 1)),
        (always, s_ref.at[pl.ds(0, 3)], u0.at[pl.ds(7, 3), :, mid], (gx, down), always, (2, 1)),
        (has_right, s_ref.at[:, :, hi8], u0.at[pl.ds(3, 4), :, left8], (gx + 1, gy), from_left, (1, 0)),
        (has_left, s_ref.at[:, :, lo8], u0.at[pl.ds(3, 4), :, right8], (gx - 1, gy), from_right, (1, 2)),
        (has_right, s_ref.at[pl.ds(2, 2), :, hi8], u0.at[pl.ds(1, 2), :, left8], (gx + 1, up), from_left, (0, 0)),
        (has_right, s_ref.at[pl.ds(0, 2), :, hi8], u0.at[pl.ds(7, 2), :, left8], (gx + 1, down), from_left, (2, 0)),
        (has_left, s_ref.at[pl.ds(2, 2), :, lo8], u0.at[pl.ds(1, 2), :, right8], (gx - 1, up), from_right, (0, 2)),
        (has_left, s_ref.at[pl.ds(0, 2), :, lo8], u0.at[pl.ds(7, 2), :, right8], (gx - 1, down), from_right, (2, 2)),
    ]
    receipts = []
    for i, (condition, src, dst, target, arrives, place) in enumerate(halo):
        big = remote(i, i, src, dst, target)
        small = remote(8 + i, 8 + i, d_ref, dn.at[place[0], place[1]], target)
        send(condition, big)
        send(condition, small)
        receipts.append((arrives, big))
        receipts.append((arrives, small))

    @pl.when(is_a)
    def _():
        remote(17, 16, ra, ra, (gx, gy)).wait_recv()

    send(is_a, remote(21, 17, ra, rb, (gx - 8, gy)))
    send(((gx == 11) | (gx == 13)) & last_z, remote(22, 18, ra, rbl, (gx - 8, up)))
    send(is_a & first_z, remote(23, 19, ra, rbr, (gx - 8, down)))

    @pl.when(is_b)
    def _():
        remote(16, 17, rb, rb, (gx, gy)).wait_recv()

    for c in range(4):
        b = gx == 1 + 2 * c
        send(b, remote(24, 20 + HY + c, rb, p0.at[HY + c, :, mid], (0 * gx, gy)))
        if c >= 1:
            send(b & jnp.logical_not(last_z), remote(25, 20 + c - 1, rb, p0.at[c - 1, :, mid], (0 * gx, up)))
        if c <= 2:
            send(b & jnp.logical_not(first_z), remote(26, 20 + 7 + c, rb, p0.at[7 + c, :, mid], (0 * gx, down)))
    for c in range(1, 4):
        b = (gx == 1 + 2 * c) & first_z

        @pl.when(b)
        def _():
            remote(20, 18, rbl, rbl, (gx, gy)).wait_recv()

        send(b, remote(27, 20 + c - 1, rbl, p0.at[c - 1, :, mid], (0 * gx, gy)))
    for c in range(3):
        b = (gx == 1 + 2 * c) & last_z

        @pl.when(b)
        def _():
            remote(23, 19, rbr, rbr, (gx, gy)).wait_recv()

        send(b, remote(28, 20 + 7 + c, rbr, p0.at[7 + c, :, mid], (0 * gx, gy)))

    @pl.when(gx == 0)
    def _():
        for r in range(ROWS):
            remote(24, 20 + r, rb, p0.at[r, :, mid], (gx, gy)).wait_recv()

    strip = pl.ds(1, 8)
    for k, (a, b) in enumerate(((64, 0), (8, 8))):
        copy = remote(29 + k, 30 + k, p0.at[strip, :, pl.ds(a, 8)], p0.at[strip, :, pl.ds(b, 8)], (1 + 0 * gx, gy))
        send(gx == 0, copy)

        @pl.when(gx == 1)
        def _(copy=copy):
            copy.wait_recv()

    own.wait()
    for condition, copy in receipts:
        @pl.when(condition)
        def _(copy=copy):
            copy.wait_recv()
    for condition, copy in sends:
        @pl.when(condition)
        def _(copy=copy):
            copy.wait_send()

    @pl.when(gx == 0)
    def _():
        @pl.loop(0, ROWS)
        def _(r):
            p0[r, :, 0:8] = p0[r, :, 64:72]
            p0[r, :, 72:80] = p0[r, :, 8:16]
            u0[r, :, 0:8] = p0[r, :, 64:72]

    @pl.when(gx == LAST)
    def _():
        @pl.loop(0, ROWS)
        def _(r):
            u0[r, :, 0:8] = u0[r, :, 64:72]
            u0[r, :, 72:80] = u0[r, :, 8:16]

    dn[1, 1] = d_ref[...]
    lane = lax.broadcasted_iota(jnp.int32, (8, NZ), 1)
    lane_f = lane.astype(jnp.float32)
    for ny in range(3):
        rows = {0: (1, 2, 3), 1: (0, 1, 2, 3), 2: (0, 1, 2)}[ny]
        base = {0: -1, 1: 3, 2: 7}[ny]
        for nx in range(3):
            spots = jnp.transpose(dn[ny, nx])
            if nx == 0:
                spots = jnp.where(from_left, spots[CX - 8:CX], -1.0)
            elif nx == 1:
                spots = spots[:CX]
            else:
                spots = jnp.where(from_right, spots[0:8], -1.0)
            start = {0: 0, 1: 8, 2: EX - 8}[nx]
            for y in rows:
                for t in range(spots.shape[0] // 8):
                    one = spots[8 * t:8 * t + 8, 2 * y:2 * y + 1]
                    two = spots[8 * t:8 * t + 8, 2 * y + 1:2 * y + 2]
                    hit = (lane_f == one) | (lane_f == two)
                    thrust[base + y, start + 8 * t:start + 8 * t + 8] = jnp.where(hit, -0.5 * THRUST_COEFF, 0.0)

    low_edge, high_edge = lane == 0, lane == NZ - 1

    def terms(which, slot, row, t):
        cells = pl.ds(pl.multiple_of(8 * t, 8), 8)
        shifted = pl.ds(pl.multiple_of(8 * t + 8, 8), 8)
        u = [st[which, slot, row, f, cells] for f in range(NF)]
        inverse = 1.0 / u[0]
        speed = [u[1] * inverse, u[2] * inverse, u[3] * inverse]
        pressure = 0.4 * (u[4] - 0.5 * (u[1] * speed[0] + u[2] * speed[1] + u[3] * speed[2]))
        total = u[4] + pressure
        flux = []
        for d in range(3):
            part = [u[1 + d], u[1] * speed[d], u[2] * speed[d], u[3] * speed[d], total * speed[d]]
            part[1 + d] = part[1 + d] + pressure
            flux.append(part)
        if which == 0:
            force = thrust[row, cells] * u[1] * jnp.abs(speed[0])
        for f in range(NF):
            ax[row, f, shifted] = u[f] + flux[0][f]
            bx[row, f, shifted] = u[f] - flux[0][f]
            ay[row, f, cells] = u[f] + flux[1][f]
            by[row, f, cells] = u[f] - flux[1][f]
            a, b = u[f] + flux[2][f], u[f] - flux[2][f]
            vertical = jnp.where(low_edge, a, pltpu.roll(a, 1, 1)) + jnp.where(high_edge, b, pltpu.roll(b, NZ - 1, 1))
            rest = 0.5 * vertical - 3.0 * u[f]
            if which == 0 and f == 1:
                rest = rest + force
            if which == 0 and f == 4:
                rest = rest + force * speed[0]
            rr[row, f, cells] = rest

    def update(which, slot, row, t, keep, take):
        cells = pl.ds(pl.multiple_of(8 * t, 8), 8)
        for f in range(NF):
            near = ax[row, f, pl.ds(8 * t + 7, 8)] + bx[row, f, pl.ds(8 * t + 9, 8)]
            near = near + (ay[row - 1, f, cells] + by[row + 1, f, cells])
            slope = 0.5 * near + rr[row, f, cells]
            fresh = st[which, slot, row, f, cells] + TIME_STEP * slope
            st[which, 1, row, f, cells] = keep * st[which, 0, row, f, cells] + take * fresh

    def stage(s, carry):
        slot = jnp.minimum(s, 1)
        keep = jnp.where(s == 0, 0.0, jnp.where(s == 1, 0.75, 1.0 / 3.0))
        take = jnp.where(s == 0, 1.0, jnp.where(s == 1, 0.25, 2.0 / 3.0))

        def advance(which, tiles):
            @pl.loop(s, ROWS - s)
            def _(row):
                @pl.loop(0, tiles)
                def _(t):
                    terms(which, slot, row, t)

            if which == 0:
                @pl.when(gx == LAST - 1)
                def _():
                    @pl.loop(s, ROWS - s)
                    def _(row):
                        bx[row, :, 80:81] = bx[row, :, 79:80]

            @pl.loop(s + 1, ROWS - 1 - s)
            def _(row):
                @pl.loop(0, tiles)
                def _(t):
                    update(which, slot, row, t, keep, take)

        @pl.when(gx <= 1)
        def _():
            advance(1, jnp.where(gx == 0, XT, 2))

        advance(0, XT)

        @pl.when(gx <= 1)
        def _():
            @pl.loop(s + 1, ROWS - 1 - s)
            def _(row):
                @pl.loop(0, jnp.where(gx == 0, XT - 1, 1))
                def _(t):
                    cells = pl.ds(pl.multiple_of(8 * t, 8), 8)
                    weight = w_ref[cells]
                    for f in range(NF):
                        value = st[0, 1, row, f, cells]
                        st[0, 1, row, f, cells] = value + weight * (st[1, 1, row, f, cells] - value)

        return carry

    lax.fori_loop(0, 3, stage, 0)
    for y in range(CY):
        o_ref[y] = st[0, 1, HY + y, :, 8:8 + CX]


def shards(density, velocity, pressure, disk_cells, disk_count, fringe_level):
    column = lax.axis_index("gx")
    with jax.named_scope("state"):
        fields = conserved_from(density, velocity, pressure)
        fields = jnp.transpose(fields, (2, 0, 1, 3))
    with jax.named_scope("disks"):
        cells = disk_cells.reshape(-1)
        slots = jnp.arange(cells.shape[0], dtype=jnp.int32)
        spots = jnp.where(slots < disk_count.reshape(()), cells % NZ, -1).astype(jnp.float32)
        spots = jnp.transpose(spots.reshape(CX, 2 * CY))
        spots = jnp.pad(spots, ((0, 0), (0, NZ - CX)), constant_values=-1.0)
    with jax.named_scope("fringe"):
        weights = fringe_level.astype(jnp.float32) / 64.0
        one, zero = jnp.ones((8,), jnp.float32), jnp.zeros((8,), jnp.float32)
        at_first = jnp.concatenate([one, weights, zero])
        at_second = jnp.concatenate([weights[CX - 8:], jnp.zeros((EX - 8,), jnp.float32)])
        weights = jnp.where(column == 0, at_first, jnp.where(column == 1, at_second, 0.0))
        weights = jnp.broadcast_to(weights[:, None], (EX, NZ))
    vmem = pl.BlockSpec(memory_space=pltpu.VMEM)
    f32 = jnp.float32
    out = pl.pallas_call(
        body,
        out_shape=jax.ShapeDtypeStruct((CY, NF, CX, NZ), f32),
        in_specs=[vmem, vmem, vmem],
        out_specs=vmem,
        scratch_shapes=[
            pltpu.VMEM((2, 2, ROWS, NF, EX, NZ), f32),
            pltpu.VMEM((ROWS, NF, EX + 16, NZ), f32),
            pltpu.VMEM((ROWS, NF, EX + 16, NZ), f32),
            pltpu.VMEM((ROWS, NF, EX, NZ), f32),
            pltpu.VMEM((ROWS, NF, EX, NZ), f32),
            pltpu.VMEM((ROWS, NF, EX, NZ), f32),
            pltpu.VMEM((ROWS, EX, NZ), f32),
            pltpu.VMEM((3, 3, 8, NZ), f32),
            pltpu.VMEM((NF, CX, NZ), f32),
            pltpu.VMEM((NF, CX, NZ), f32),
            pltpu.VMEM((NF, CX, NZ), f32),
            pltpu.VMEM((NF, CX, NZ), f32),
            pltpu.SemaphoreType.DMA,
            pltpu.SemaphoreType.DMA((32,)),
            pltpu.SemaphoreType.DMA((32,)),
        ],
        compiler_params=pltpu.CompilerParams(collective_id=0, has_side_effects=True),
    )(fields, spots, weights)
    return jnp.transpose(out, (1, 2, 0, 3))


def solution(mesh):
    in_specs = (
        P("gx", "gy", None),
        P(None, "gx", "gy", None),
        P("gx", "gy", None),
        P("gx", "gy", None),
        P("gx", "gy"),
        P(),
    )
    out_specs = P(None, "gx", "gy", None)
    return jax.shard_map(shards, mesh=mesh, in_specs=in_specs, out_specs=out_specs, check_vma=False)
```

time: 430 us -> 157 us (0.37)
  the two profiles are of different devices: /device:TPU:56 before, /device:TPU:24 now
where the time goes in v1:
time: 157 us
  Pallas kernels  148 us (94%)
  local copies, waits for them, and re-layouts  7.07 us (5%)
    pallas_call x1, Pallas kernels, shards(): pl.pallas_call(body, out_shape=jax.ShapeDtypeStruct((CY, NF, CX, NZ), f32...  148 us

profile of v1, /device:TPU:24, one launch (start us, length us, event | category | flops | bytes accessed | tf_op | source)
XLA Modules:
  0.0 156.6 jit_solution(15004144572600426620)
XLA Ops:
  0.0 0.0 copy-start
  0.0 1.1 fusion.6
  1.1 0.0 copy-done
  1.2 0.0 copy-start.2
  1.2 0.9 copy-done.2
  2.1 0.0 copy-start.1
  2.2 0.0 copy-start.4
  2.2 0.7 copy-done.4
  2.9 0.1 slice.19
  2.9 0.1 broadcast_select_fusion.1
  3.0 0.0 copy-start.3
  3.0 0.7 broadcast_in_dim.17.w_ref
  3.7 0.5 broadcast.36
  4.2 0.0 copy-done.3
  4.2 0.6 reduce.3
  4.9 0.1 reshape.13
  5.0 0.1 copy.32
  5.7 0.6 pad.5.d_ref
  6.3 0.0 copy-done.1
  6.3 147.9 %shard_map.64 = f32[4,5,64,128]{3,2,1,0:T(8,128)} custom-call(f32[4,5,64,128]{3,2,1,0:T(8,128)} %bitcast.41, f32[8,128]{1,0:T(8,128)} %pad.5.d_ref, f32[80,128]{1,0:T(8,128)} %broadcast_in_dim.17.w_ref), custom_call_target="tpu_custom_call" | custom-call | tf_op jit(solution)/shard_map/pallas_call | solution.py:334
  154.2 2.3 %copy.35 = f32[5,64,4,128]{3,2,1,0:T(4,128)} copy(f32[5,64,4,128]{3,1,0,2:T(8,128)} %bitcast.40) | data formatting | bytes 1310720 | tf_op jit(solution)/shard_map/transpose | solution.py:358
  (9 shorter events, 0.1 us)
Async XLA Ops:
  0.0 1.1 copy-start
  1.2 0.9 copy-start.2
  2.1 4.2 %copy-start.1 = (f32[5,64,4,128]{3,1,0,2:T(8,128)}, f32[5,64,4,128]{3,1,0,2:T(8,128)S(1)}, u32[]{:S(2)}) copy-start(f32[5,64,4,128]{3,1,0,2:T(8,128)S(1)} %bitcast_dynamic-update-slice_fusion.3) | copy-start | bytes 1966084
  2.2 0.7 copy-start.4
  3.0 1.2 copy-start.3

commit v2 on v1

v2 whole, which is shorter than its diff:
```python
import jax
import jax.numpy as jnp
from jax import lax
from jax.experimental import pallas as pl
from jax.experimental.pallas import tpu as pltpu
from jax.sharding import PartitionSpec as P

TIME_STEP = 0.05
THRUST_COEFF = 0.75
MEAN_WIND = 1.0
MESH = pl.DeviceIdType.MESH

CX, CY, NZ, NF = 64, 4, 128, 5
HY = 3
ROWS = CY + 2 * HY
XT = CX // 8 + 2
EX = 8 * XT
LAST = 15
Z_LO = 16


def conserved_from(density, velocity, pressure):
    stream = velocity[0] + MEAN_WIND
    energy = pressure / 0.4 + 0.5 * density * (
        stream * stream + velocity[1] * velocity[1] + velocity[2] * velocity[2]
    )
    return jnp.stack(
        [density, density * stream, density * velocity[1], density * velocity[2], energy]
    )


HX = 3
SUB = 4
PIECE = CX // SUB


def body(s_ref, d_ref, count_ref, level_ref, o_ref, st, ax, bx, ay, by, rr, thrust, wt, dd, dn, ra, rb, rbl, rbr,
         go_sem, local_sem, send_sem, recv_sem):
    gx, gy = lax.axis_index("gx"), lax.axis_index("gy")
    up, down = lax.rem(gy + 1, 64), lax.rem(gy + 63, 64)
    z_lo = lax.rem(gy, Z_LO)
    first_z, last_z = z_lo == 0, z_lo == Z_LO - 1
    has_right, has_left = gx <= LAST - 2, (gx >= 1) & (gx <= LAST - 1)
    from_left, from_right = (gx >= 1) & (gx <= LAST - 1), gx <= LAST - 2
    u0 = st.at[0, 0]
    p0 = st.at[1, 0]
    zero = 0 * gx

    sends = []
    numbers = iter(range(1000))

    def remote(send_index, recv, src, dst, target):
        return pltpu.make_async_remote_copy(
            src_ref=src, dst_ref=dst, send_sem=send_sem.at[send_index], recv_sem=recv_sem.at[recv],
            device_id=target, device_id_type=MESH,
        )

    def send(condition, recv, src, dst, target):
        copy = remote(next(numbers), recv, src, dst, target)
        sends.append((condition, copy))

        @pl.when(condition)
        def _():
            copy.start()

        return copy

    def arrived(recv, dst):
        remote(0, recv, dst, dst, (gx, gy)).wait_recv()

    barrier = pltpu.get_barrier_semaphore()

    def tell(condition, device):
        @pl.when(condition)
        def _():
            pl.semaphore_signal(barrier, inc=1, device_id=device, device_id_type=MESH)

    always = gx >= 0
    is_source = gx == LAST
    near_source = (9, 11, 13, 14)
    near_fringe = (1, 3, 5, 7)
    for c in range(4):
        a, b = near_source[c], near_fringe[c]
        tell(gx == b, (a + zero, gy))
        if c >= 1:
            tell((gx == b) & first_z, (a + zero, down))
        if c <= 2:
            tell((gx == b) & last_z, (a + zero, up))
    at_step = first_z | last_z
    not_first, not_last = jnp.logical_not(first_z), jnp.logical_not(last_z)
    tell(not_last, (gx, up))
    tell(not_first, (gx, down))
    for near, close in ((gy, always), (up, not_last), (down, not_first)):
        tell(from_left & (close | (gx == 8)), (gx - 1, near))
        tell(from_right & (close | (gx == 7)), (gx + 1, near))
    half = jnp.where(gx < 8, 0, 8)
    speaker = jnp.where(gx < 8, 7, 8)
    tell(last_z, (speaker, up))
    tell(first_z, (speaker, down))
    tell(at_step & (gx != speaker), (speaker, gy))
    for c in range(4):
        tell(gx == near_source[c], (LAST + zero, gy))
        tell(gx == 0, (near_fringe[c] + zero, gy))

    own = pltpu.make_async_copy(s_ref, u0.at[pl.ds(HY, CY), :, pl.ds(8, CX)], local_sem)
    own.start()

    slot = NZ * lax.broadcasted_iota(jnp.int32, (4, NZ), 0) + lax.broadcasted_iota(jnp.int32, (4, NZ), 1)
    spots = jnp.where(slot < count_ref[0, 0], d_ref[...] & (NZ - 1), -1).astype(jnp.float32)
    dd[0:4] = spots
    dd[4:8] = spots

    def yes(condition):
        return jnp.where(condition, 1, 0)

    is_a = (gx == 9) | (gx == 11) | (gx == 13) | (gx == 14)
    is_b = (gx == 1) | (gx == 3) | (gx == 5) | (gx == 7)
    near_count = 3 - yes(at_step)
    expected = near_count - 1 + 4 * yes(is_source) + yes(is_a) + yes(is_b)
    expected += yes(has_right) * jnp.where(gx == 7, 3, near_count)
    expected += yes(has_left) * jnp.where(gx == 8, 3, near_count)
    expected += 15 * yes(at_step & (gx == speaker))
    expected += yes(is_a & (gx >= 11) & last_z) + yes(is_a & (gx <= 13) & first_z)
    pl.semaphore_wait(barrier, expected)
    for k in range(8):
        @pl.when(at_step & (gx == speaker) & (gx != half + k))
        def _(k=k):
            pl.semaphore_signal(go_sem, inc=1, device_id=(half + k, gy), device_id_type=MESH)

    at_ra, at_rb, at_rbl, at_rbr, at_p = 16, 16 + SUB, 16 + 2 * SUB, 16 + 3 * SUB, 16 + 4 * SUB
    at_strip = at_p + ROWS * SUB
    pieces = [pl.ds(PIECE * j, PIECE) for j in range(SUB)]
    inner = [pl.ds(8 + PIECE * j, PIECE) for j in range(SUB)]

    for j in range(SUB):
        for c in range(4):
            send(is_source, at_ra + j, s_ref.at[c, :, pieces[j]], ra.at[:, pieces[j]], (near_source[c] + zero, gy))

    @pl.when(is_a)
    def _():
        for j in range(SUB):
            arrived(at_ra + j, ra.at[:, pieces[j]])
    target = gx - 8 + yes(gx == 14)
    for j in range(SUB):
        piece = ra.at[:, pieces[j]]
        send(is_a, at_rb + j, piece, rb.at[:, pieces[j]], (target, gy))
        send(is_a & (gx >= 11) & last_z, at_rbl + j, piece, rbl.at[:, pieces[j]], (target, up))
        send(is_a & (gx <= 13) & first_z, at_rbr + j, piece, rbr.at[:, pieces[j]], (target, down))
    rows_out = sends[4 * SUB:]
    del sends[4 * SUB:]
    for condition, copy in rows_out:
        @pl.when(condition)
        def _(copy=copy):
            copy.wait_send()

    mid = pl.ds(8, CX)
    def edge(first, rows, low, cells):
        src = s_ref.at[pl.ds(first, rows), :, pl.ds(0, cells) if low else pl.ds(CX - cells, cells)]
        return src, pl.ds(EX - 8, cells) if low else pl.ds(8 - cells, cells)

    halo = [
        (always, s_ref.at[pl.ds(1, 3)], u0.at[pl.ds(0, 3), :, mid], (gx, up), always, (0, 1)),
        (always, s_ref.at[pl.ds(0, 3)], u0.at[pl.ds(7, 3), :, mid], (gx, down), always, (2, 1)),
    ]
    for low in (False, True):
        condition, arrives, other, nx = (has_left, from_right, gx - 1, 2) if low else (has_right, from_left, gx + 1, 0)
        src, cells = edge(0, CY, low, HX)
        halo.append((condition, src, u0.at[pl.ds(HY, CY), :, cells], (other, gy), arrives, (1, nx)))
        src, cells = edge(2, 2, low, HX)
        halo.append((condition, src, u0.at[pl.ds(1, 2), :, cells], (other, up), arrives, (0, nx)))
        src, cells = edge(0, 2, low, HX)
        halo.append((condition, src, u0.at[pl.ds(7, 2), :, cells], (other, down), arrives, (2, nx)))
    receipts = []

    def send_halo(i, condition):
        wanted, src, dst, target, arrives, place = halo[i]
        copy = send(wanted & condition, i, src, dst, target)
        small = send(wanted & condition, 8 + i, dd, dn.at[place[0], place[1]], target)
        return [(arrives, copy), (arrives, small)]

    for i in range(len(halo)):
        far = last_z if i in (0, 3, 6) else first_z
        receipts += send_halo(i, always) if i in (2, 5) else send_halo(i, jnp.logical_not(far))
    @pl.when(at_step & (gx != speaker))
    def _():
        pl.semaphore_wait(go_sem, 1)

    for i in (0, 1, 3, 4, 6, 7):
        send_halo(i, last_z if i in (0, 3, 6) else first_z)

    for j in range(SUB):
        @pl.when(is_b)
        def _(j=j):
            arrived(at_rb + j, rb.at[:, pieces[j]])

        for c in range(4):
            row = HY + c
            send(gx == near_fringe[c], at_p + row * SUB + j, rb.at[:, pieces[j]], p0.at[row, :, inner[j]], (zero, gy))
    for j in range(SUB):
        @pl.when(is_b & (gx >= 3) & first_z)
        def _(j=j):
            arrived(at_rbl + j, rbl.at[:, pieces[j]])

        @pl.when(is_b & (gx <= 5) & last_z)
        def _(j=j):
            arrived(at_rbr + j, rbr.at[:, pieces[j]])

        for c in range(4):
            if c >= 1:
                row = c - 1
                send((gx == near_fringe[c]) & first_z, at_p + row * SUB + j, rbl.at[:, pieces[j]], p0.at[row, :, inner[j]], (zero, gy))
            if c <= 2:
                row = 7 + c
                send((gx == near_fringe[c]) & last_z, at_p + row * SUB + j, rbr.at[:, pieces[j]], p0.at[row, :, inner[j]], (zero, gy))

    for j in range(SUB):
        for c in range(4):
            here = p0.at[HY + c, :, inner[j]]

            @pl.when(gx == 0)
            def _(j=j, c=c, here=here):
                arrived(at_p + (HY + c) * SUB + j, here)

            if c >= 1:
                send((gx == 0) & jnp.logical_not(last_z), at_p + (c - 1) * SUB + j, here, p0.at[c - 1, :, inner[j]], (zero, up))
            if c <= 2:
                send((gx == 0) & jnp.logical_not(first_z), at_p + (7 + c) * SUB + j, here, p0.at[7 + c, :, inner[j]], (zero, down))

    @pl.when(gx == 0)
    def _():
        for j in range(SUB):
            for row in (0, 1, 2, 7, 8, 9):
                arrived(at_p + row * SUB + j, p0.at[row, :, inner[j]])

    strip = pl.ds(1, 8)
    for k, (a, b) in enumerate(((64, 0), (8, 8))):
        copy = send(gx == 0, at_strip + k, p0.at[strip, :, pl.ds(a, 8)], p0.at[strip, :, pl.ds(b, 8)], (1 + zero, gy))

        @pl.when(gx == 1)
        def _(copy=copy):
            copy.wait_recv()

    own.wait()
    for condition, copy in receipts:
        @pl.when(condition)
        def _(copy=copy):
            copy.wait_recv()
    for condition, copy in sends:
        @pl.when(condition)
        def _(copy=copy):
            copy.wait_send()

    @pl.when(gx == 0)
    def _():
        @pl.loop(0, ROWS)
        def _(r):
            p0[r, :, 0:8] = p0[r, :, 64:72]
            p0[r, :, 72:80] = p0[r, :, 8:16]
            u0[r, :, 0:8] = p0[r, :, 64:72]

    @pl.when(gx == LAST)
    def _():
        @pl.loop(0, ROWS)
        def _(r):
            u0[r, :, 0:8] = u0[r, :, 64:72]
            u0[r, :, 72:80] = u0[r, :, 8:16]

    lane = lax.broadcasted_iota(jnp.int32, (8, NZ), 1)
    lane_f = lane.astype(jnp.float32)
    sublane = lax.broadcasted_iota(jnp.int32, (8, NZ), 0)

    def disks(place, tile):
        line = dd if place == (1, 1) else dn.at[place[0], place[1]]
        wide = jnp.broadcast_to(line[tile // 2:tile // 2 + 1], (8, NZ))
        value = wide
        for k in range(8):
            shift = 64 * (tile % 2) + 8 * k
            if shift:
                value = jnp.where(sublane == k, pltpu.roll(wide, NZ - shift, 1), value)
        return value

    for ny in range(3):
        rows = {0: (1, 2, 3), 1: (0, 1, 2, 3), 2: (0, 1, 2)}[ny]
        base = {0: -1, 1: 3, 2: 7}[ny]
        for t in range(XT):
            if t == 0:
                spots = jnp.where(from_left, disks((ny, 0), CX // 8 - 1), -1.0)
            elif t == XT - 1:
                spots = jnp.where(from_right, disks((ny, 2), 0), -1.0)
            else:
                spots = disks((ny, 1), t - 1)
            for y in rows:
                one, two = spots[:, 2 * y:2 * y + 1], spots[:, 2 * y + 1:2 * y + 2]
                hit = (lane_f == one) | (lane_f == two)
                thrust[base + y, 8 * t:8 * t + 8] = jnp.where(hit, -0.5 * THRUST_COEFF, 0.0)

    def weights(tile):
        value = jnp.zeros((8, NZ), jnp.float32)
        for k in range(8):
            level = level_ref[8 * tile + k].astype(jnp.float32) / 64.0
            value = jnp.where(sublane == k, level, value)
        return value

    @pl.when(gx == 0)
    def _():
        wt[0:8] = jnp.ones((8, NZ), jnp.float32)
        for t in range(CX // 8):
            wt[8 + 8 * t:16 + 8 * t] = weights(t)

    @pl.when(gx == 1)
    def _():
        wt[0:8] = weights(CX // 8 - 1)

    low_edge, high_edge = lane == 0, lane == NZ - 1

    def terms(which, slot, row, t):
        cells, shifted = pl.ds(8 * t, 8), pl.ds(8 * t + 8, 8)
        u = [st[which, slot, row, f, cells] for f in range(NF)]
        inverse = 1.0 / u[0]
        speed = [u[1] * inverse, u[2] * inverse, u[3] * inverse]
        pressure = 0.4 * (u[4] - 0.5 * (u[1] * speed[0] + u[2] * speed[1] + u[3] * speed[2]))
        total = u[4] + pressure
        flux = []
        for d in range(3):
            part = [u[1 + d], u[1] * speed[d], u[2] * speed[d], u[3] * speed[d], total * speed[d]]
            part[1 + d] = part[1 + d] + pressure
            flux.append(part)
        if which == 0:
            force = thrust[row, cells] * u[1] * jnp.abs(speed[0])
        for f in range(NF):
            ax[row, f, shifted] = u[f] + flux[0][f]
            bx[row, f, shifted] = u[f] - flux[0][f]
            ay[row, f, cells] = u[f] + flux[1][f]
            by[row, f, cells] = u[f] - flux[1][f]
            a, b = u[f] + flux[2][f], u[f] - flux[2][f]
            vertical = jnp.where(low_edge, a, pltpu.roll(a, 1, 1)) + jnp.where(high_edge, b, pltpu.roll(b, NZ - 1, 1))
            rest = 0.5 * vertical - 3.0 * u[f]
            if which == 0 and f == 1:
                rest = rest + force
            if which == 0 and f == 4:
                rest = rest + force * speed[0]
            rr[row, f, cells] = rest

    def edge_terms(which, slot, row, t, sign, ref):
        cells = pl.ds(8 * t, 8)
        u = [st[which, slot, row, f, cells] for f in range(NF)]
        inverse = 1.0 / u[0]
        speed = u[2] * inverse
        square = (u[1] * u[1] + u[2] * u[2] + u[3] * u[3]) * inverse
        pressure = 0.4 * (u[4] - 0.5 * square)
        flux = [u[2], u[1] * speed, u[2] * speed + pressure, u[3] * speed, (u[4] + pressure) * speed]
        for f in range(NF):
            ref[row, f, cells] = u[f] + sign * flux[f]

    def update(which, slot, row, tiles, keep, take):
        for f in range(NF):
            done = []
            for t in range(tiles):
                cells = pl.ds(8 * t, 8)
                near = ax[row, f, pl.ds(8 * t + 7, 8)] + bx[row, f, pl.ds(8 * t + 9, 8)]
                near = near + (ay[row - 1, f, cells] + by[row + 1, f, cells])
                slope = 0.5 * near + rr[row, f, cells]
                fresh = st[which, slot, row, f, cells] + TIME_STEP * slope
                done.append(keep * st[which, 0, row, f, cells] + take * fresh)
            for t in range(tiles):
                st[which, 1, row, f, pl.ds(8 * t, 8)] = done[t]

    def stage(s, carry):
        slot = jnp.minimum(s, 1)
        keep = jnp.where(s == 0, 0.0, jnp.where(s == 1, 0.75, 1.0 / 3.0))
        take = jnp.where(s == 0, 1.0, jnp.where(s == 1, 0.25, 2.0 / 3.0))

        def advance(which, tiles):
            for t in range(tiles):
                edge_terms(which, slot, s, t, 1.0, ay)
            for t in range(tiles):
                edge_terms(which, slot, ROWS - 1 - s, t, -1.0, by)

            @pl.loop(s + 1, ROWS - 1 - s)
            def _(row):
                for t in range(tiles):
                    terms(which, slot, row, t)

            if which == 0:
                @pl.when(gx == LAST - 1)
                def _():
                    @pl.loop(s + 1, ROWS - 1 - s)
                    def _(row):
                        bx[row, :, 80:81] = bx[row, :, 79:80]

            @pl.loop(s + 1, ROWS - 1 - s)
            def _(row):
                update(which, slot, row, tiles, keep, take)

        @pl.when(gx == 0)
        def _():
            advance(1, XT)

        @pl.when(gx == 1)
        def _():
            advance(1, 2)

        advance(0, XT)

        def blend(tiles):
            @pl.loop(s + 1, ROWS - 1 - s)
            def _(row):
                for t in range(tiles):
                    cells = pl.ds(8 * t, 8)
                    weight = wt[cells]
                    for f in range(NF):
                        value = st[0, 1, row, f, cells]
                        st[0, 1, row, f, cells] = value + weight * (st[1, 1, row, f, cells] - value)

        @pl.when(gx == 0)
        def _():
            blend(XT - 1)

        @pl.when(gx == 1)
        def _():
            blend(1)

        return carry

    lax.fori_loop(0, 3, stage, 0)
    for y in range(CY):
        o_ref[y] = st[0, 1, HY + y, :, 8:8 + CX]


def shards(density, velocity, pressure, disk_cells, disk_count, fringe_level):
    with jax.named_scope("state"):
        fields = conserved_from(density, velocity, pressure)
        fields = jnp.transpose(fields, (2, 0, 1, 3))
    cells = disk_cells.reshape(4, NZ)
    vmem = pl.BlockSpec(memory_space=pltpu.VMEM)
    smem = pl.BlockSpec(memory_space=pltpu.SMEM)
    f32 = jnp.float32
    out = pl.pallas_call(
        body,
        out_shape=jax.ShapeDtypeStruct((CY, NF, CX, NZ), f32),
        in_specs=[vmem, vmem, smem, smem],
        out_specs=vmem,
        scratch_shapes=[
            pltpu.VMEM((2, 2, ROWS, NF, EX, NZ), f32),
            pltpu.VMEM((ROWS, NF, EX + 16, NZ), f32),
            pltpu.VMEM((ROWS, NF, EX + 16, NZ), f32),
            pltpu.VMEM((ROWS, NF, EX, NZ), f32),
            pltpu.VMEM((ROWS, NF, EX, NZ), f32),
            pltpu.VMEM((ROWS, NF, EX, NZ), f32),
            pltpu.VMEM((ROWS, EX, NZ), f32),
            pltpu.VMEM((EX, NZ), f32),
            pltpu.VMEM((8, NZ), f32),
            pltpu.VMEM((3, 3, 8, NZ), f32),
            pltpu.VMEM((NF, CX, NZ), f32),
            pltpu.VMEM((NF, CX, NZ), f32),
            pltpu.VMEM((NF, CX, NZ), f32),
            pltpu.VMEM((NF, CX, NZ), f32),
            pltpu.SemaphoreType.REGULAR,
            pltpu.SemaphoreType.DMA,
            pltpu.SemaphoreType.DMA((160,)),
            pltpu.SemaphoreType.DMA((16 + (4 + ROWS) * SUB + 2,)),
        ],
        compiler_params=pltpu.CompilerParams(collective_id=0, has_side_effects=True),
    )(fields, cells, disk_count, fringe_level)
    return jnp.transpose(out, (1, 2, 0, 3))


def solution(mesh):
    in_specs = (
        P("gx", "gy", None),
        P(None, "gx", "gy", None),
        P("gx", "gy", None),
        P("gx", "gy", None),
        P("gx", "gy"),
        P(),
    )
    out_specs = P(None, "gx", "gy", None)
    return jax.shard_map(shards, mesh=mesh, in_specs=in_specs, out_specs=out_specs, check_vma=False)
```

time: 157 us -> 94 us (0.60)
  Pallas kernels: 148 us -> 88.4 us
  local copies, waits for them, and re-layouts: 7.07 us -> 4.51 us
    pallas_call x1, Pallas kernels: 148 us -> 88.4 us  [shards(): pl.pallas_call(body, out_shape=jax.ShapeDtypeStruct((CY, NF, CX, NZ), f32...]
where the time goes in v2:
time: 94 us; the launch traced here: 93.7 us
  Pallas kernels  88.4 us (94%)
  local copies, waits for them, and re-layouts  4.51 us (5%)
    pallas_call x1, Pallas kernels, shards(): pl.pallas_call(body, out_shape=jax.ShapeDtypeStruct((CY, NF, CX, NZ), f32...  88.4 us
    transpose x1, local copies, waits for them, and re-layouts, shards(): return jnp.transpose(out, (1, 2, 0, 3))  2.35 us

profile of v2, /device:TPU:24, one launch (start us, length us, event | category | flops | bytes accessed | tf_op | source)
XLA Modules:
  0.0 93.7 jit_solution(3275561524177626724)
XLA Ops:
  0.0 0.0 copy-start
  0.0 1.1 %fusion.2 = (f32[1,64,4,128]{3,2,1,0:T(4,128)S(1)}, f32[1,64,4,128]{3,2,1,0:T(4,128)S(1)}, f32[1,64,4,128]{3,2,1,0:T(4,128)S(1)}) fusion(f32[3,64,4,128]{3,2,1,0:T(4,128)} %param.7), kind=kLoop, calls=%fused_computation.11 | loop fusion | bytes 786432 | tf_op jit(solution)/shard_map/state/slice | solution.py:28
  1.1 0.0 copy-done
  1.2 0.0 copy-start.2
  1.2 0.9 copy-done.2
  2.1 0.0 copy-start.1
  2.8 0.2 copy-done.1
  3.0 88.4 %shard_map.64 = f32[4,5,64,128]{3,2,1,0:T(8,128)} custom-call(f32[4,5,64,128]{3,2,1,0:T(8,128)} %bitcast.38, s32[4,128]{1,0:T(4,128)} %bitcast.39, s32[1,1]{1,0:T(1,128)S(6)} %copy.54.count_ref, s32[64]{0:T(128)} %level_ref.1), custom_call_target="tpu_custom_call" | custom-call | tf_op jit(solution)/shard_map/pallas_call | solution.py:438
  91.4 2.3 %copy.19 = f32[5,64,4,128]{3,2,1,0:T(4,128)} copy(f32[5,64,4,128]{3,1,0,2:T(8,128)} %bitcast.37) | data formatting | bytes 1310720 | tf_op jit(solution)/shard_map/transpose | solution.py:465
  (5 shorter events, 0.1 us)
Async XLA Ops:
  0.0 1.1 %copy-start = (f32[64,4,128]{2,1,0:T(4,128)S(1)}, f32[64,4,128]{2,1,0:T(4,128)}, u32[]{:S(2)}) copy-start(f32[64,4,128]{2,1,0:T(4,128)} %param.6) | copy-start | bytes 393220
  1.2 0.9 copy-start.2
  2.1 0.8 copy-start.1

commit v3 on v2

--- a/solution.py
+++ b/solution.py
@@ -34,7 +34,7 @@
 PIECE = CX // SUB
 
 
-def body(s_ref, d_ref, count_ref, level_ref, o_ref, st, ax, bx, ay, by, rr, thrust, wt, dd, dn, ra, rb, rbl, rbr,
+def body(s_ref, d_ref, count_ref, level_ref, o_ref, st, pp, ax, bx, ay, by, rr, thrust, wt, dd, dn, ra, rb, rbl, rbr,
          go_sem, local_sem, send_sem, recv_sem):
     gx, gy = lax.axis_index("gx"), lax.axis_index("gy")
     up, down = lax.rem(gy + 1, 64), lax.rem(gy + 63, 64)
@@ -42,8 +42,9 @@
     first_z, last_z = z_lo == 0, z_lo == Z_LO - 1
     has_right, has_left = gx <= LAST - 2, (gx >= 1) & (gx <= LAST - 1)
     from_left, from_right = (gx >= 1) & (gx <= LAST - 1), gx <= LAST - 2
-    u0 = st.at[0, 0]
-    p0 = st.at[1, 0]
+    u0 = st.at[0]
+    p0 = pp.at[0]
+    held = (st, pp)
     zero = 0 * gx
 
     sends = []
@@ -101,6 +102,10 @@
     for c in range(4):
         tell(gx == near_source[c], (LAST + zero, gy))
         tell(gx == 0, (near_fringe[c] + zero, gy))
+        if c >= 1:
+            tell((gx == 0) & not_first, (near_fringe[c] + zero, down))
+        if c <= 2:
+            tell((gx == 0) & not_last, (near_fringe[c] + zero, up))
 
     own = pltpu.make_async_copy(s_ref, u0.at[pl.ds(HY, CY), :, pl.ds(8, CX)], local_sem)
     own.start()
@@ -121,6 +126,7 @@
     expected += yes(has_left) * jnp.where(gx == 8, 3, near_count)
     expected += 15 * yes(at_step & (gx == speaker))
     expected += yes(is_a & (gx >= 11) & last_z) + yes(is_a & (gx <= 13) & first_z)
+    expected += yes(is_b & (gx >= 3) & not_last) + yes(is_b & (gx <= 5) & not_first)
     pl.semaphore_wait(barrier, expected)
     for k in range(8):
         @pl.when(at_step & (gx == speaker) & (gx != half + k))
@@ -181,12 +187,15 @@
     for i in range(len(halo)):
         far = last_z if i in (0, 3, 6) else first_z
         receipts += send_halo(i, always) if i in (2, 5) else send_halo(i, jnp.logical_not(far))
-    @pl.when(at_step & (gx != speaker))
-    def _():
-        pl.semaphore_wait(go_sem, 1)
-
-    for i in (0, 1, 3, 4, 6, 7):
-        send_halo(i, last_z if i in (0, 3, 6) else first_z)
+    def send_far(who):
+        @pl.when(at_step & (gx != speaker) & who)
+        def _():
+            pl.semaphore_wait(go_sem, 1)
+
+        for i in (0, 1, 3, 4, 6, 7):
+            send_halo(i, (last_z if i in (0, 3, 6) else first_z) & who)
+
+    send_far(always)
 
     for j in range(SUB):
         @pl.when(is_b)
@@ -195,7 +204,12 @@
 
         for c in range(4):
             row = HY + c
-            send(gx == near_fringe[c], at_p + row * SUB + j, rb.at[:, pieces[j]], p0.at[row, :, inner[j]], (zero, gy))
+            here, piece = gx == near_fringe[c], rb.at[:, pieces[j]]
+            send(here, at_p + row * SUB + j, piece, p0.at[row, :, inner[j]], (zero, gy))
+            if c >= 1:
+                send(here & not_last, at_p + (c - 1) * SUB + j, piece, p0.at[c - 1, :, inner[j]], (zero, up))
+            if c <= 2:
+                send(here & not_first, at_p + (7 + c) * SUB + j, piece, p0.at[7 + c, :, inner[j]], (zero, down))
     for j in range(SUB):
         @pl.when(is_b & (gx >= 3) & first_z)
         def _(j=j):
@@ -213,23 +227,10 @@
                 row = 7 + c
                 send((gx == near_fringe[c]) & last_z, at_p + row * SUB + j, rbr.at[:, pieces[j]], p0.at[row, :, inner[j]], (zero, gy))
 
-    for j in range(SUB):
-        for c in range(4):
-            here = p0.at[HY + c, :, inner[j]]
-
-            @pl.when(gx == 0)
-            def _(j=j, c=c, here=here):
-                arrived(at_p + (HY + c) * SUB + j, here)
-
-            if c >= 1:
-                send((gx == 0) & jnp.logical_not(last_z), at_p + (c - 1) * SUB + j, here, p0.at[c - 1, :, inner[j]], (zero, up))
-            if c <= 2:
-                send((gx == 0) & jnp.logical_not(first_z), at_p + (7 + c) * SUB + j, here, p0.at[7 + c, :, inner[j]], (zero, down))
-
     @pl.when(gx == 0)
     def _():
         for j in range(SUB):
-            for row in (0, 1, 2, 7, 8, 9):
+            for row in range(ROWS):
                 arrived(at_p + row * SUB + j, p0.at[row, :, inner[j]])
 
     strip = pl.ds(1, 8)
@@ -240,82 +241,12 @@
         def _(copy=copy):
             copy.wait_recv()
 
-    own.wait()
-    for condition, copy in receipts:
-        @pl.when(condition)
-        def _(copy=copy):
-            copy.wait_recv()
-    for condition, copy in sends:
-        @pl.when(condition)
-        def _(copy=copy):
-            copy.wait_send()
-
-    @pl.when(gx == 0)
-    def _():
-        @pl.loop(0, ROWS)
-        def _(r):
-            p0[r, :, 0:8] = p0[r, :, 64:72]
-            p0[r, :, 72:80] = p0[r, :, 8:16]
-            u0[r, :, 0:8] = p0[r, :, 64:72]
-
-    @pl.when(gx == LAST)
-    def _():
-        @pl.loop(0, ROWS)
-        def _(r):
-            u0[r, :, 0:8] = u0[r, :, 64:72]
-            u0[r, :, 72:80] = u0[r, :, 8:16]
-
     lane = lax.broadcasted_iota(jnp.int32, (8, NZ), 1)
-    lane_f = lane.astype(jnp.float32)
-    sublane = lax.broadcasted_iota(jnp.int32, (8, NZ), 0)
-
-    def disks(place, tile):
-        line = dd if place == (1, 1) else dn.at[place[0], place[1]]
-        wide = jnp.broadcast_to(line[tile // 2:tile // 2 + 1], (8, NZ))
-        value = wide
-        for k in range(8):
-            shift = 64 * (tile % 2) + 8 * k
-            if shift:
-                value = jnp.where(sublane == k, pltpu.roll(wide, NZ - shift, 1), value)
-        return value
-
-    for ny in range(3):
-        rows = {0: (1, 2, 3), 1: (0, 1, 2, 3), 2: (0, 1, 2)}[ny]
-        base = {0: -1, 1: 3, 2: 7}[ny]
-        for t in range(XT):
-            if t == 0:
-                spots = jnp.where(from_left, disks((ny, 0), CX // 8 - 1), -1.0)
-            elif t == XT - 1:
-                spots = jnp.where(from_right, disks((ny, 2), 0), -1.0)
-            else:
-                spots = disks((ny, 1), t - 1)
-            for y in rows:
-                one, two = spots[:, 2 * y:2 * y + 1], spots[:, 2 * y + 1:2 * y + 2]
-                hit = (lane_f == one) | (lane_f == two)
-                thrust[base + y, 8 * t:8 * t + 8] = jnp.where(hit, -0.5 * THRUST_COEFF, 0.0)
-
-    def weights(tile):
-        value = jnp.zeros((8, NZ), jnp.float32)
-        for k in range(8):
-            level = level_ref[8 * tile + k].astype(jnp.float32) / 64.0
-            value = jnp.where(sublane == k, level, value)
-        return value
-
-    @pl.when(gx == 0)
-    def _():
-        wt[0:8] = jnp.ones((8, NZ), jnp.float32)
-        for t in range(CX // 8):
-            wt[8 + 8 * t:16 + 8 * t] = weights(t)
-
-    @pl.when(gx == 1)
-    def _():
-        wt[0:8] = weights(CX // 8 - 1)
-
     low_edge, high_edge = lane == 0, lane == NZ - 1
 
     def terms(which, slot, row, t):
         cells, shifted = pl.ds(8 * t, 8), pl.ds(8 * t + 8, 8)
-        u = [st[which, slot, row, f, cells] for f in range(NF)]
+        u = [held[which][slot, row, f, cells] for f in range(NF)]
         inverse = 1.0 / u[0]
         speed = [u[1] * inverse, u[2] * inverse, u[3] * inverse]
         pressure = 0.4 * (u[4] - 0.5 * (u[1] * speed[0] + u[2] * speed[1] + u[3] * speed[2]))
@@ -343,7 +274,7 @@
 
     def edge_terms(which, slot, row, t, sign, ref):
         cells = pl.ds(8 * t, 8)
-        u = [st[which, slot, row, f, cells] for f in range(NF)]
+        u = [held[which][slot, row, f, cells] for f in range(NF)]
         inverse = 1.0 / u[0]
         speed = u[2] * inverse
         square = (u[1] * u[1] + u[2] * u[2] + u[3] * u[3]) * inverse
@@ -352,7 +283,7 @@
         for f in range(NF):
             ref[row, f, cells] = u[f] + sign * flux[f]
 
-    def update(which, slot, row, tiles, keep, take):
+    def update(which, slot, out, row, tiles, keep, take):
         for f in range(NF):
             done = []
             for t in range(tiles):
@@ -360,47 +291,126 @@
                 near = ax[row, f, pl.ds(8 * t + 7, 8)] + bx[row, f, pl.ds(8 * t + 9, 8)]
                 near = near + (ay[row - 1, f, cells] + by[row + 1, f, cells])
                 slope = 0.5 * near + rr[row, f, cells]
-                fresh = st[which, slot, row, f, cells] + TIME_STEP * slope
-                done.append(keep * st[which, 0, row, f, cells] + take * fresh)
+                fresh = held[which][slot, row, f, cells] + TIME_STEP * slope
+                done.append(keep * held[which][0, row, f, cells] + take * fresh)
             for t in range(tiles):
-                st[which, 1, row, f, pl.ds(8 * t, 8)] = done[t]
-
-    def stage(s, carry):
-        slot = jnp.minimum(s, 1)
+                held[which][out, row, f, pl.ds(8 * t, 8)] = done[t]
+
+    def advance(s, which, slot, out, tiles):
         keep = jnp.where(s == 0, 0.0, jnp.where(s == 1, 0.75, 1.0 / 3.0))
         take = jnp.where(s == 0, 1.0, jnp.where(s == 1, 0.25, 2.0 / 3.0))
 
-        def advance(which, tiles):
+        for t in range(tiles):
+            edge_terms(which, slot, s, t, 1.0, ay)
+        for t in range(tiles):
+            edge_terms(which, slot, ROWS - 1 - s, t, -1.0, by)
+
+        @pl.loop(s + 1, ROWS - 1 - s)
+        def _(row):
             for t in range(tiles):
-                edge_terms(which, slot, s, t, 1.0, ay)
-            for t in range(tiles):
-                edge_terms(which, slot, ROWS - 1 - s, t, -1.0, by)
-
-            @pl.loop(s + 1, ROWS - 1 - s)
-            def _(row):
-                for t in range(tiles):
-                    terms(which, slot, row, t)
-
-            if which == 0:
-                @pl.when(gx == LAST - 1)
-                def _():
-                    @pl.loop(s + 1, ROWS - 1 - s)
-                    def _(row):
-                        bx[row, :, 80:81] = bx[row, :, 79:80]
-
-            @pl.loop(s + 1, ROWS - 1 - s)
-            def _(row):
-                update(which, slot, row, tiles, keep, take)
-
-        @pl.when(gx == 0)
-        def _():
-            advance(1, XT)
-
-        @pl.when(gx == 1)
-        def _():
-            advance(1, 2)
-
-        advance(0, XT)
+                terms(which, slot, row, t)
+
+        if which == 0:
+            @pl.when(gx == LAST - 1)
+            def _():
+                @pl.loop(s + 1, ROWS - 1 - s)
+                def _(row):
+                    bx[row, :, 80:81] = bx[row, :, 79:80]
+
+        @pl.loop(s + 1, ROWS - 1 - s)
+        def _(row):
+            update(which, slot, out, row, tiles, keep, take)
+
+    def precursor(tiles):
+        def one(s, carry):
+            advance(s, 1, s, s + 1, tiles)
+            return carry
+
+        lax.fori_loop(0, 3, one, 0)
+
+    @pl.when(gx == 0)
+    def _():
+        @pl.loop(0, ROWS)
+        def _(r):
+            p0[r, :, 0:8] = p0[r, :, 64:72]
+            p0[r, :, 72:80] = p0[r, :, 8:16]
+
+        precursor(XT)
+
+    @pl.when(gx == 1)
+    def _():
+        precursor(2)
+
+    own.wait()
+    for condition, copy in receipts:
+        @pl.when(condition)
+        def _(copy=copy):
+            copy.wait_recv()
+    for condition, copy in sends:
+        @pl.when(condition)
+        def _(copy=copy):
+            copy.wait_send()
+
+    @pl.when(gx == 0)
+    def _():
+        @pl.loop(0, ROWS)
+        def _(r):
+            u0[r, :, 0:8] = p0[r, :, 64:72]
+
+    @pl.when(gx == LAST)
+    def _():
+        @pl.loop(0, ROWS)
+        def _(r):
+            u0[r, :, 0:8] = u0[r, :, 64:72]
+            u0[r, :, 72:80] = u0[r, :, 8:16]
+
+    lane_f = lane.astype(jnp.float32)
+    sublane = lax.broadcasted_iota(jnp.int32, (8, NZ), 0)
+
+    def disks(place, tile):
+        line = dd if place == (1, 1) else dn.at[place[0], place[1]]
+        wide = jnp.broadcast_to(line[tile // 2:tile // 2 + 1], (8, NZ))
+        value = wide
+        for k in range(8):
+            shift = 64 * (tile % 2) + 8 * k
+            if shift:
+                value = jnp.where(sublane == k, pltpu.roll(wide, NZ - shift, 1), value)
+        return value
+
+    for ny in range(3):
+        rows = {0: (1, 2, 3), 1: (0, 1, 2, 3), 2: (0, 1, 2)}[ny]
+        base = {0: -1, 1: 3, 2: 7}[ny]
+        for t in range(XT):
+            if t == 0:
+                spots = jnp.where(from_left, disks((ny, 0), CX // 8 - 1), -1.0)
+            elif t == XT - 1:
+                spots = jnp.where(from_right, disks((ny, 2), 0), -1.0)
+            else:
+                spots = disks((ny, 1), t - 1)
+            for y in rows:
+                one, two = spots[:, 2 * y:2 * y + 1], spots[:, 2 * y + 1:2 * y + 2]
+                hit = (lane_f == one) | (lane_f == two)
+                thrust[base + y, 8 * t:8 * t + 8] = jnp.where(hit, -0.5 * THRUST_COEFF, 0.0)
+
+    def weights(tile):
+        value = jnp.zeros((8, NZ), jnp.float32)
+        for k in range(8):
+            level = level_ref[8 * tile + k].astype(jnp.float32) / 64.0
+            value = jnp.where(sublane == k, level, value)
+        return value
+
+    @pl.when(gx == 0)
+    def _():
+        wt[0:8] = jnp.ones((8, NZ), jnp.float32)
+        for t in range(CX // 8):
+            wt[8 + 8 * t:16 + 8 * t] = weights(t)
+
+    @pl.when(gx == 1)
+    def _():
+        wt[0:8] = weights(CX // 8 - 1)
+
+    def stage(s, carry):
+        advance(s, 0, jnp.minimum(s, 1), 1, XT)
 
         def blend(tiles):
             @pl.loop(s + 1, ROWS - 1 - s)
@@ -409,8 +419,8 @@
                     cells = pl.ds(8 * t, 8)
                     weight = wt[cells]
                     for f in range(NF):
-                        value = st[0, 1, row, f, cells]
-                        st[0, 1, row, f, cells] = value + weight * (st[1, 1, row, f, cells] - value)
+                        value = st[1, row, f, cells]
+                        st[1, row, f, cells] = value + weight * (pp[s + 1, row, f, cells] - value)
 
         @pl.when(gx == 0)
         def _():
@@ -424,7 +434,7 @@
 
     lax.fori_loop(0, 3, stage, 0)
     for y in range(CY):
-        o_ref[y] = st[0, 1, HY + y, :, 8:8 + CX]
+        o_ref[y] = st[1, HY + y, :, 8:8 + CX]
 
 
 def shards(density, velocity, pressure, disk_cells, disk_count, fringe_level):
@@ -441,7 +451,8 @@
         in_specs=[vmem, vmem, smem, smem],
         out_specs=vmem,
         scratch_shapes=[
-            pltpu.VMEM((2, 2, ROWS, NF, EX, NZ), f32),
+            pltpu.VMEM((2, ROWS, NF, EX, NZ), f32),
+            pltpu.VMEM((4, ROWS, NF, EX, NZ), f32),
             pltpu.VMEM((ROWS, NF, EX + 16, NZ), f32),
             pltpu.VMEM((ROWS, NF, EX + 16, NZ), f32),
             pltpu.VMEM((ROWS, NF, EX, NZ), f32),
@@ -457,7 +468,7 @@
             pltpu.VMEM((NF, CX, NZ), f32),
             pltpu.SemaphoreType.REGULAR,
             pltpu.SemaphoreType.DMA,
-            pltpu.SemaphoreType.DMA((160,)),
+            pltpu.SemaphoreType.DMA((220,)),
             pltpu.SemaphoreType.DMA((16 + (4 + ROWS) * SUB + 2,)),
         ],
         compiler_params=pltpu.CompilerParams(collective_id=0, has_side_effects=True),

time: 94 us -> 89.9 us (0.956)
  Pallas kernels: 88.4 us -> 84 us
    pallas_call x1, Pallas kernels: 88.4 us -> 84 us  [shards(): pl.pallas_call(body, out_shape=jax.ShapeDtypeStruct((CY, NF, CX, NZ), f32...]
where the time goes in v3:
time: 89.9 us; the launch traced here: 89.3 us
  Pallas kernels  84 us (93%)
  local copies, waits for them, and re-layouts  4.51 us (5%)
    pallas_call x1, Pallas kernels, shards(): pl.pallas_call(body, out_shape=jax.ShapeDtypeStruct((CY, NF, CX, NZ), f32...  84 us
    transpose x1, local copies, waits for them, and re-layouts, shards(): return jnp.transpose(out, (1, 2, 0, 3))  2.35 us

profile of v3, /device:TPU:24, one launch (start us, length us, event | category | flops | bytes accessed | tf_op | source)
XLA Modules:
  0.0 89.3 jit_solution(4007556971319776805)
XLA Ops:
  0.0 0.0 copy-start
  0.0 1.1 %fusion.2 = (f32[1,64,4,128]{3,2,1,0:T(4,128)S(1)}, f32[1,64,4,128]{3,2,1,0:T(4,128)S(1)}, f32[1,64,4,128]{3,2,1,0:T(4,128)S(1)}) fusion(f32[3,64,4,128]{3,2,1,0:T(4,128)} %param.7), kind=kLoop, calls=%fused_computation.11 | loop fusion | bytes 786432 | tf_op jit(solution)/shard_map/state/slice | solution.py:28
  1.1 0.0 copy-done
  1.2 0.0 copy-start.2
  1.2 0.9 copy-done.2
  2.1 0.0 copy-start.1
  2.8 0.2 copy-done.1
  3.0 84.0 %shard_map.64 = f32[4,5,64,128]{3,2,1,0:T(8,128)} custom-call(f32[4,5,64,128]{3,2,1,0:T(8,128)} %bitcast.38, s32[4,128]{1,0:T(4,128)} %bitcast.39, s32[1,1]{1,0:T(1,128)S(6)} %copy.54.count_ref, s32[64]{0:T(128)} %level_ref.1), custom_call_target="tpu_custom_call" | custom-call | tf_op jit(solution)/shard_map/pallas_call | solution.py:448
  86.9 2.3 %copy.19 = f32[5,64,4,128]{3,2,1,0:T(4,128)} copy(f32[5,64,4,128]{3,1,0,2:T(8,128)} %bitcast.37) | data formatting | bytes 1310720 | tf_op jit(solution)/shard_map/transpose | solution.py:476
  (5 shorter events, 0.1 us)
Async XLA Ops:
  0.0 1.1 %copy-start = (f32[64,4,128]{2,1,0:T(4,128)S(1)}, f32[64,4,128]{2,1,0:T(4,128)}, u32[]{:S(2)}) copy-start(f32[64,4,128]{2,1,0:T(4,128)} %param.6) | copy-start | bytes 393220
  1.2 0.9 %copy-start.2 = (f32[64,4,128]{2,1,0:T(4,128)S(1)}, f32[64,4,128]{2,1,0:T(4,128)}, u32[]{:S(2)}) copy-start(f32[64,4,128]{2,1,0:T(4,128)} %param.8) | copy-start | bytes 393220
  2.1 0.8 copy-start.1

commit v4 on v3

--- a/solution.py
+++ b/solution.py
@@ -434,7 +434,7 @@
 
     lax.fori_loop(0, 3, stage, 0)
     for y in range(CY):
-        o_ref[y] = st[1, HY + y, :, 8:8 + CX]
+        o_ref[:, y] = st[1, HY + y, :, 8:8 + CX]
 
 
 def shards(density, velocity, pressure, disk_cells, disk_count, fringe_level):
@@ -447,7 +447,7 @@
     f32 = jnp.float32
     out = pl.pallas_call(
         body,
-        out_shape=jax.ShapeDtypeStruct((CY, NF, CX, NZ), f32),
+        out_shape=jax.ShapeDtypeStruct((NF, CY, CX, NZ), f32),
         in_specs=[vmem, vmem, smem, smem],
         out_specs=vmem,
         scratch_shapes=[
@@ -473,7 +473,7 @@
         ],
         compiler_params=pltpu.CompilerParams(collective_id=0, has_side_effects=True),
     )(fields, cells, disk_count, fringe_level)
-    return jnp.transpose(out, (1, 2, 0, 3))
+    return jnp.transpose(out, (0, 2, 1, 3))
 
 
 def solution(mesh):

time: 89.9 us -> 89.9 us (level)
  no operation moved by 1% of the time
where the time goes in v4:
time: 89.9 us; the launch traced here: 89.3 us
  Pallas kernels  84 us (93%)
  local copies, waits for them, and re-layouts  4.51 us (5%)
    pallas_call x1, Pallas kernels, shards(): pl.pallas_call(body, out_shape=jax.ShapeDtypeStruct((NF, CY, CX, NZ), f32...  84 us
    transpose x1, local copies, waits for them, and re-layouts, shards(): return jnp.transpose(out, (0, 2, 1, 3))  2.35 us

profile of v4, /device:TPU:24, one launch (start us, length us, event | category | flops | bytes accessed | tf_op | source)
XLA Modules:
  0.0 89.3 jit_solution(12759845446008395710)
XLA Ops:
  0.0 0.0 copy-start
  0.0 1.1 %fusion.2 = (f32[1,64,4,128]{3,2,1,0:T(4,128)S(1)}, f32[1,64,4,128]{3,2,1,0:T(4,128)S(1)}, f32[1,64,4,128]{3,2,1,0:T(4,128)S(1)}) fusion(f32[3,64,4,128]{3,2,1,0:T(4,128)} %param.7), kind=kLoop, calls=%fused_computation.11 | loop fusion | bytes 786432 | tf_op jit(solution)/shard_map/state/slice | solution.py:28
  1.1 0.0 copy-done
  1.2 0.0 copy-start.2
  1.2 0.9 copy-done.2
  2.1 0.0 copy-start.1
  2.8 0.2 copy-done.1
  3.0 84.0 %shard_map.64 = f32[5,4,64,128]{3,2,1,0:T(8,128)} custom-call(f32[4,5,64,128]{3,2,1,0:T(8,128)} %bitcast.38, s32[4,128]{1,0:T(4,128)} %bitcast.39, s32[1,1]{1,0:T(1,128)S(6)} %copy.54.count_ref, s32[64]{0:T(128)} %level_ref.1), custom_call_target="tpu_custom_call" | custom-call | tf_op jit(solution)/shard_map/pallas_call | solution.py:448
  86.9 2.3 %copy.19 = f32[5,64,4,128]{3,2,1,0:T(4,128)} copy(f32[5,64,4,128]{3,1,2,0:T(8,128)} %bitcast.37) | data formatting | bytes 1310720 | tf_op jit(solution)/shard_map/transpose | solution.py:476
  (5 shorter events, 0.1 us)
Async XLA Ops:
  0.0 1.1 %copy-start = (f32[64,4,128]{2,1,0:T(4,128)S(1)}, f32[64,4,128]{2,1,0:T(4,128)}, u32[]{:S(2)}) copy-start(f32[64,4,128]{2,1,0:T(4,128)} %param.6) | copy-start | bytes 393220
  1.2 0.9 %copy-start.2 = (f32[64,4,128]{2,1,0:T(4,128)S(1)}, f32[64,4,128]{2,1,0:T(4,128)}, u32[]{:S(2)}) copy-start(f32[64,4,128]{2,1,0:T(4,128)} %param.8) | copy-start | bytes 393220
  2.1 0.8 copy-start.1

commit v5 on v3

--- a/solution.py
+++ b/solution.py
@@ -152,13 +152,6 @@
         send(is_a, at_rb + j, piece, rb.at[:, pieces[j]], (target, gy))
         send(is_a & (gx >= 11) & last_z, at_rbl + j, piece, rbl.at[:, pieces[j]], (target, up))
         send(is_a & (gx <= 13) & first_z, at_rbr + j, piece, rbr.at[:, pieces[j]], (target, down))
-    rows_out = sends[4 * SUB:]
-    del sends[4 * SUB:]
-    for condition, copy in rows_out:
-        @pl.when(condition)
-        def _(copy=copy):
-            copy.wait_send()
-
     mid = pl.ds(8, CX)
     def edge(first, rows, low, cells):
         src = s_ref.at[pl.ds(first, rows), :, pl.ds(0, cells) if low else pl.ds(CX - cells, cells)]

time: 89.9 us -> 89.4 us (level)
  no operation moved by 1% of the time
where the time goes in v5:
time: 89.4 us; the launch traced here: 89.2 us
  Pallas kernels  83.9 us (94%)
  local copies, waits for them, and re-layouts  4.51 us (5%)
    pallas_call x1, Pallas kernels, shards(): pl.pallas_call(body, out_shape=jax.ShapeDtypeStruct((CY, NF, CX, NZ), f32...  83.9 us
    transpose x1, local copies, waits for them, and re-layouts, shards(): return jnp.transpose(out, (1, 2, 0, 3))  2.35 us

profile of v5, /device:TPU:24, one launch (start us, length us, event | category | flops | bytes accessed | tf_op | source)
XLA Modules:
  0.0 89.2 jit_solution(12252167363438096692)
XLA Ops:
  0.0 0.0 copy-start
  0.0 1.1 %fusion.2 = (f32[1,64,4,128]{3,2,1,0:T(4,128)S(1)}, f32[1,64,4,128]{3,2,1,0:T(4,128)S(1)}, f32[1,64,4,128]{3,2,1,0:T(4,128)S(1)}) fusion(f32[3,64,4,128]{3,2,1,0:T(4,128)} %param.7), kind=kLoop, calls=%fused_computation.11 | loop fusion | bytes 786432 | tf_op jit(solution)/shard_map/state/slice | solution.py:28
  1.1 0.0 copy-done
  1.2 0.0 copy-start.2
  1.2 0.9 copy-done.2
  2.1 0.0 copy-start.1
  2.8 0.2 copy-done.1
  3.0 83.9 %shard_map.64 = f32[4,5,64,128]{3,2,1,0:T(8,128)} custom-call(f32[4,5,64,128]{3,2,1,0:T(8,128)} %bitcast.38, s32[4,128]{1,0:T(4,128)} %bitcast.39, s32[1,1]{1,0:T(1,128)S(6)} %copy.54.count_ref, s32[64]{0:T(128)} %level_ref.1), custom_call_target="tpu_custom_call" | custom-call | tf_op jit(solution)/shard_map/pallas_call | solution.py:441
  86.8 2.3 %copy.19 = f32[5,64,4,128]{3,2,1,0:T(4,128)} copy(f32[5,64,4,128]{3,1,0,2:T(8,128)} %bitcast.37) | data formatting | bytes 1310720 | tf_op jit(solution)/shard_map/transpose | solution.py:469
  (5 shorter events, 0.1 us)
Async XLA Ops:
  0.0 1.1 %copy-start = (f32[64,4,128]{2,1,0:T(4,128)S(1)}, f32[64,4,128]{2,1,0:T(4,128)}, u32[]{:S(2)}) copy-start(f32[64,4,128]{2,1,0:T(4,128)} %param.6) | copy-start | bytes 393220
  1.2 0.9 %copy-start.2 = (f32[64,4,128]{2,1,0:T(4,128)S(1)}, f32[64,4,128]{2,1,0:T(4,128)}, u32[]{:S(2)}) copy-start(f32[64,4,128]{2,1,0:T(4,128)} %param.8) | copy-start | bytes 393220
  2.1 0.8 copy-start.1
